TPU v7x, 32 devices: a whole 2x2x4 slice. The times are simulated.
32 devices in a mesh: section: 4 (over z), token: 4 (over x, core), feature: 2 (over y).
Axes of the slice: x: 2, y: 2, z: 4, core: 2. Of those that a mesh axis runs over, the one named last changes fastest.
Arguments:
- residual: bfloat16 [4, 2048, 4608], P('section', 'token'), may hold values from -6 to 6
- encoder: bfloat16 [4, 4608, 8192], P('section', None, 'feature'), may hold values from -0.09375 to 0.09375
- encoder_bias: float32 [4, 8192], P('section', 'feature'), may hold values from -0.6 to 0.3
- decoder: bfloat16 [4, 4, 8192, 4608], P('section', 'token', None, 'feature'), may hold values from -0.125 to 0.125
- active: int32 [4, 32, 16], P('section'), may hold values from 0 to 3
Outputs:
- activations: bfloat16 [4, 2048, 8192], P('section', 'token', 'feature')
- reconstruction: bfloat16 [4, 2048, 4608], P('token', 'section', 'feature')
Inputs may be any that keep to these rules, and one draw needn't show every extreme that they name: Which of the 4 blocks of a group is active, for each section and tile of 64 tokens.
All inputs are finite; a program needn't handle non-finite values.
Results may differ from a plain program's by a relative error of at most 0.0049.
Values may be sent and summed in bfloat16 or wider, within the bound.
A program may use at most 256 MiB of HBM per device.

v0:
```python
import jax
import jax.numpy as jnp
from jax import lax
from jax.sharding import PartitionSpec as P

G = 16
BPG = 4
TILE = 64
BLOCK = 128


def decode_tiles(block_codes, picked, weights):
    flags = (picked[..., None] == jnp.arange(BPG, dtype=jnp.int32)).astype(jnp.bfloat16)
    dense = block_codes[:, :, :, :, None, :] * flags[:, :, None, :, :, None]
    return jnp.einsum("qptgbc,qgbcd->qptd", dense, weights, preferred_element_type=jnp.float32)


def body(residual, encoder, encoder_bias, decoder, active):
    section = lax.axis_index("section")
    token_place = lax.axis_index("token")
    feature_place = lax.axis_index("feature")
    feature_count = lax.axis_size("feature")
    rows_here = residual.shape[1]
    width_local = decoder.shape[3]
    groups_local = G // feature_count
    tile_count = rows_here // TILE
    hidden = jnp.dot(residual[0], encoder[0], preferred_element_type=jnp.float32) + encoder_bias[0]
    feature_codes = jax.nn.relu(hidden).astype(jnp.bfloat16)
    own_active = lax.dynamic_slice(
        active[0],
        (token_place * tile_count, feature_place * groups_local),
        (tile_count, groups_local),
    )
    own_flags = (own_active[..., None] == jnp.arange(BPG, dtype=jnp.int32)).astype(jnp.bfloat16)
    blocks = feature_codes.reshape(tile_count, TILE, groups_local, BPG, BLOCK)
    compact = jnp.einsum("ptgbc,pgb->ptgc", blocks, own_flags, preferred_element_type=jnp.float32)
    compact = compact.astype(jnp.bfloat16).reshape(rows_here, groups_local * BLOCK)
    dec_groups = decoder[0, 0].reshape(G, BPG, BLOCK, width_local)
    in_range = (token_place >= section).astype(jnp.float32)
    all_groups = lax.all_gather(compact, "feature", axis=1, tiled=True)
    arrived = lax.all_gather(all_groups, "token", axis=0, tiled=True)
    row_count = arrived.shape[0]
    piece_tiles = row_count // TILE
    block_codes = arrived.reshape(1, piece_tiles, TILE, G, BLOCK)
    picked = active[0][None]
    decoded = decode_tiles(block_codes, picked, dec_groups[None]).reshape(row_count, width_local)
    partial_value = decoded
    partial_value = partial_value * in_range
    rebuilt = lax.psum_scatter(partial_value, "section", scatter_dimension=0, tiled=True).astype(
        jnp.bfloat16
    )
    return (feature_codes[None], rebuilt[None])


def solution(mesh):
    placed = (
        P("section", "token", None),
        P("section", None, "feature"),
        P("section", "feature"),
        P("section", "token", None, "feature"),
        P("section", None, None),
    )
    return jax.shard_map(
        body,
        mesh=mesh,
        in_specs=placed,
        out_specs=(P("section", "token", "feature"), P("token", "section", "feature")),
        check_vma=False,
    )
```

profile of v0, /device:TPU:0, one launch (start us, length us, event | category | flops | bytes accessed | tf_op | source)
XLA Modules:
  0.0 588.4 jit_solution(12981778055123432967)
XLA Ops:
  7.2 0.0 all-gather.3.cloned.1.call-start
  7.2 0.8 constant_dynamic-slice_fusion
  8.0 0.1 copy.16
  8.1 0.1 fusion.17
  8.1 26.2 %maximum_convert_fusion = bf16[512,4096]{1,0:T(8,128)(2,1)} fusion(bf16[1,4608,4096]{2,1,0:T(8,128)(2,1)} %param.6, bf16[1,512,4608]{2,1,0:T(8,128)(2,1)} %param.5, f32[4096]{0:T(1024)} %bitcast.50), kind=kOutput, calls=%fused_computation.8 | convolution fusion | flops 19333644288 | bytes 46678016 | tf_op jit(solution)/shard_map/dot_general | solution.py:27
  34.4 7.7 %reshape.40 = bf16[8,64,8,4,128]{4,3,2,1,0:T(4,128)(2,1)} reshape(bf16[512,4096]{1,0:T(8,128)(2,1)} %maximum_convert_fusion) | data formatting | bytes 8388608 | tf_op jit(solution)/shard_map/reshape | solution.py:35
  42.1 4.5 fusion.14
  46.6 1.2 copy.30
  47.8 1.2 copy.31
  49.1 0.0 all-gather.3.cloned.1.call-update
  49.1 0.0 all-gather.5.cloned.1.call-start
  49.1 35.9 %all-gather.3.cloned.1.call-done = bf16[512,2048]{1,0:T(8,128)(2,1)} async-done(((bf16[512,1024]{1,0:T(8,128)(2,1)}), bf16[512,2048]{1,0:T(8,128)(2,1)}) %all-gather.3.cloned.1.call-update) | async-done | bytes 2097168 | tf_op jit(solution)/shard_map/all_gather | solution.py:40
  85.1 0.0 all-gather.5.cloned.1.call-update
  85.1 0.2 reduce-scatter.2.cloned.1.call-start
  85.3 0.0 copy-done
  85.4 0.3 mul.46
  85.7 0.5 mul.47
  86.2 58.8 %all-gather.5.cloned.1.call-done = bf16[2048,2048]{1,0:T(8,128)(2,1)} async-done(((bf16[512,2048]{1,0:T(8,128)(2,1)}), bf16[2048,2048]{1,0:T(8,128)(2,1)}) %all-gather.5.cloned.1.call-update) | async-done | bytes 8388624 | tf_op jit(solution)/shard_map/all_gather | solution.py:41
  144.9 9.8 %copy.18 = bf16[256,8,16,128]{3,2,1,0:T(8,128)(2,1)} copy(bf16[256,8,16,128]{3,1,2,0:T(8,128)(2,1)} %bitcast.43) | data formatting | bytes 16777216
  154.7 8.9 %copy.10 = bf16[2048,128,16]{1,0,2:T(8,128)(2,1)} copy(bf16[2048,128,16]{1,2,0:T(8,128)(2,1)} %bitcast.42) | data formatting | bytes 16777216 | tf_op jit(solution)/shard_map/mul | solution.py:14
  163.6 100.3 %bitcast_multiply_fusion = f32[2048,2304]{1,0:T(8,128)} fusion(bf16[16,4,128,2304]{3,2,1,0:T(8,128)(2,1)} %bitcast.49, bf16[2048,4,16]{0,2,1:T(8,128)(2,1)S(1)} %mul.47, bf16[2048,128,16]{1,0,2:T(8,128)(2,1)} %copy.10, f32[]{:T(128)S(6)} %convert_element_type.30), kind=kOutput, calls=%fused_computation.5 | convolution fusion | flops 77330907136 | bytes 65273860 | tf_op jit(solution)/shard_map/qptgbc,qgbcd->qptd/dot_general | solution.py:15
  263.8 0.0 reduce-scatter.2.cloned.1.call-update
  263.8 314.1 %reduce-scatter.2.cloned.1.call-done = f32[512,2304]{1,0:T(8,128)} async-done(((f32[2048,2304]{1,0:T(8,128)}), f32[512,2304]{1,0:T(8,128)}) %reduce-scatter.2.cloned.1.call-update) | async-done | bytes 4718608 | tf_op jit(solution)/shard_map/reduce_scatter | solution.py:49
  577.9 4.0 convert_bitcast_fusion
  (2 shorter events, 0.0 us)
Async XLA Ops:
  7.2 77.9 %all-gather.3.cloned.1.call-start = ((), (), s32[]{:S(2)}) async-start(), calls=%async_computation.1 | async-start | bytes 3145728 | tf_op jit(solution)/shard_map/all_gather | solution.py:40
  42.1 43.3 %copy-start = (s32[1,32,16]{1,2,0:T(8,128)S(1)}, s32[1,32,16]{1,2,0:T(8,128)}, u32[]{:S(2)}) copy-start(s32[1,32,16]{1,2,0:T(8,128)} %param.9) | copy-start | bytes 6148
  49.1 95.8 %all-gather.5.cloned.1.call-start = ((), (), s32[]{:S(2)}) async-start(), calls=%async_computation.2 | async-start | bytes 10485760 | tf_op jit(solution)/shard_map/all_gather | solution.py:41
  85.1 492.8 %reduce-scatter.2.cloned.1.call-start = ((), (), s32[]{:S(2)}) async-start(), calls=%async_computation.3 | async-start | bytes 23592960 | tf_op jit(solution)/shard_map/reduce_scatter | solution.py:49
Sparse Core Ops, SparseCore 0:
  49.2 35.8 all-gather.2
  86.6 58.2 all-gather.4
  264.0 313.9 reduce-scatter.1
where the time goes:
time: 589 us; the launch traced here: 588 us
  waiting for transfers between devices  409 us (69%)
  matrix products  131 us (22%)
  local copies, waits for them, and re-layouts  30.4 us (5%)
  between operations  13.8 us (2%)
    reduce_scatter x1, waiting for transfers between devices, body(): lax.psum_scatter(partial_value, 'section', scatter_dimension=0, tiled=True)  314 us
    dot_general x1, matrix products, decode_tiles(): jnp.einsum('qptgbc,qgbcd->qptd', dense, weights, preferred_element_type=j...  100 us
    all_gather x1, waiting for transfers between devices, body(): arrived = lax.all_gather(all_groups, 'token', axis=0, tiled=True)  58.8 us
    all_gather x1, waiting for transfers between devices, body(): all_groups = lax.all_gather(compact, 'feature', axis=1, tiled=True)  35.9 us
    dot_general x1, matrix products, body(): jnp.dot(residual[0], encoder[0], preferred_element_type=jnp.float32)  26.2 us
  transfers between devices with their start and end apart: 3, of which 3 were waited for; matrix products, arithmetic and copies ran while one was open for 0% of the time, Pallas kernels for 0%

commit v1 on v0

--- a/solution.py
+++ b/solution.py
@@ -7,6 +7,16 @@
 BPG = 4
 TILE = 64
 BLOCK = 128
+
+
+def around_the_ring(x, axis, d):
+    size = lax.axis_size(axis)
+    held, blocks = (x, [x])
+    for _ in range(size - 1):
+        held = lax.ppermute(held, axis, [(i, (i + 1) % size) for i in range(size)])
+        blocks.insert(0, held)
+    merged = jnp.concatenate(blocks, axis=d)
+    return jnp.roll(merged, (lax.axis_index(axis) + 1) * x.shape[d], axis=d)
 
 
 def decode_tiles(block_codes, picked, weights):
@@ -38,7 +48,7 @@
     dec_groups = decoder[0, 0].reshape(G, BPG, BLOCK, width_local)
     in_range = (token_place >= section).astype(jnp.float32)
     all_groups = lax.all_gather(compact, "feature", axis=1, tiled=True)
-    arrived = lax.all_gather(all_groups, "token", axis=0, tiled=True)
+    arrived = around_the_ring(all_groups, "token", 0)
     row_count = arrived.shape[0]
     piece_tiles = row_count // TILE
     block_codes = arrived.reshape(1, piece_tiles, TILE, G, BLOCK)

time: 589 us -> 640 us (1.087)
  local copies, waits for them, and re-layouts: 30.4 us -> 64.1 us
  waiting for transfers between devices: 409 us -> 426 us
    ppermute x0 -> x3, waiting for transfers between devices: none -> 76.2 us  [around_the_ring(): held = lax.ppermute(held, axis, [(i, (i + 1) % size) for i in range(size)])]
    all_gather x1 -> x0, waiting for transfers between devices: 58.8 us -> none  [body(): arrived = lax.all_gather(all_groups, 'token', axis=0, tiled=True)]
    unnamed x5 -> x19, local copies, waits for them, and re-layouts: 11.1 us -> 43.3 us
  transfers between devices with their start and end apart: 3 -> 5, of which waited for: 3 -> 5; matrix products, arithmetic and copies ran while one was open for 0% -> 0% of each run, Pallas kernels for 0% -> 0%
where the time goes in v1:
time: 640 us
  waiting for transfers between devices  426 us (67%)
  matrix products  131 us (20%)
  local copies, waits for them, and re-layouts  64.1 us (10%)
  between operations  14.1 us (2%)
    reduce_scatter x1, waiting for transfers between devices, body(): lax.psum_scatter(partial_value, 'section', scatter_dimension=0, tiled=True)  314 us
    dot_general x1, matrix products, decode_tiles(): jnp.einsum('qptgbc,qgbcd->qptd', dense, weights, preferred_element_type=j...  100 us
    ppermute x3, waiting for transfers between devices, around_the_ring(): held = lax.ppermute(held, axis, [(i, (i + 1) % size) for i in range(size)])  76.2 us
    unnamed x19, local copies, waits for them, and re-layouts  43.3 us
    all_gather x1, waiting for transfers between devices, body(): all_groups = lax.all_gather(compact, 'feature', axis=1, tiled=True)  35.9 us
    dot_general x1, matrix products, body(): jnp.dot(residual[0], encoder[0], preferred_element_type=jnp.float32)  26.2 us
  transfers between devices with their start and end apart: 5, of which 5 were waited for; matrix products, arithmetic and copies ran while one was open for 0% of the time, Pallas kernels for 0%

profile of v1, /device:TPU:0, one launch (start us, length us, event | category | flops | bytes accessed | tf_op | source)
XLA Modules:
  0.0 639.6 jit_solution(4212900111778756848)
XLA Ops:
  8.1 26.2 %maximum_convert_fusion = bf16[512,4096]{1,0:T(8,128)(2,1)} fusion(bf16[1,4608,4096]{2,1,0:T(8,128)(2,1)} %param.6, bf16[1,512,4608]{2,1,0:T(8,128)(2,1)} %param.5, f32[4096]{0:T(1024)} %bitcast.50), kind=kOutput, calls=%fused_computation.9 | convolution fusion | flops 19333644288 | bytes 46678016 | tf_op jit(solution)/shard_map/dot_general | solution.py:37
  34.4 7.7 %reshape.40 = bf16[8,64,8,4,128]{4,3,2,1,0:T(4,128)(2,1)} reshape(bf16[512,4096]{1,0:T(8,128)(2,1)} %maximum_convert_fusion) | data formatting | bytes 8388608 | tf_op jit(solution)/shard_map/reshape | solution.py:45
  42.1 4.5 fusion.14
  46.6 1.2 copy.30
  47.8 1.2 copy.31
  49.2 35.9 %all-gather.2.cloned.1.call-done = bf16[512,2048]{1,0:T(8,128)(2,1)} async-done(((bf16[512,1024]{1,0:T(8,128)(2,1)}), bf16[512,2048]{1,0:T(8,128)(2,1)}) %all-gather.2.cloned.1.call-update) | async-done | bytes 2097168 | tf_op jit(solution)/shard_map/all_gather | solution.py:50
  85.1 25.7 %collective-permute-done = bf16[512,2048]{1,0:T(8,128)(2,1)S(1)} collective-permute-done((bf16[512,2048]{1,0:T(8,128)(2,1)}, bf16[512,2048]{1,0:T(8,128)(2,1)S(1)}, u32[]{:S(2)}, u32[]{:S(2)}) %collective-permute-start) | collective-permute-done | bytes 2097184 | tf_op jit(solution)/shard_map/ppermute | solution.py:16
  110.8 1.3 copy-done.1
  112.1 25.6 %collective-permute-done.1 = bf16[512,2048]{1,0:T(8,128)(2,1)} collective-permute-done((bf16[512,2048]{1,0:T(8,128)(2,1)S(1)}, bf16[512,2048]{1,0:T(8,128)(2,1)}, u32[]{:S(2)}, u32[]{:S(2)}) %collective-permute-start.1) | collective-permute-done | bytes 2097184 | tf_op jit(solution)/shard_map/ppermute | solution.py:16
  138.5 24.9 %collective-permute-done.2 = bf16[512,2048]{1,0:T(8,128)(2,1)} collective-permute-done((bf16[512,2048]{1,0:T(8,128)(2,1)}, bf16[512,2048]{1,0:T(8,128)(2,1)}, u32[]{:S(2)}, u32[]{:S(2)}) %collective-permute-start.2) | collective-permute-done | bytes 2097184 | tf_op jit(solution)/shard_map/ppermute | solution.py:16
  163.4 3.2 constant_dynamic-update-slice_fusion.7
  166.6 3.2 constant_dynamic-update-slice_fusion.6
  169.8 3.2 constant_dynamic-update-slice_fusion.5
  172.9 3.2 constant_dynamic-update-slice_fusion.4
  176.1 3.2 constant_dynamic-update-slice_fusion.3
  179.3 3.2 constant_dynamic-update-slice_fusion.2
  182.5 1.5 constant_dynamic-update-slice_fusion.1
  183.9 1.4 constant_dynamic-update-slice_fusion
  185.4 10.3 %dynamic-slice_bitcast_fusion = bf16[256,8,16,128]{3,1,2,0:T(8,128)(2,1)} fusion(bf16[4096,2048]{1,0:T(8,128)(2,1)} %constant_dynamic-update-slice_fusion, s32[]{:T(128)S(6)} %select_n.22), kind=kLoop, calls=%fused_computation.8 | loop fusion | bytes 16777220
  195.7 9.8 %copy.18 = bf16[256,8,16,128]{3,2,1,0:T(8,128)(2,1)} copy(bf16[256,8,16,128]{3,1,2,0:T(8,128)(2,1)} %dynamic-slice_bitcast_fusion) | data formatting | bytes 16777216
  205.5 8.9 %copy.10 = bf16[2048,128,16]{1,0,2:T(8,128)(2,1)} copy(bf16[2048,128,16]{1,2,0:T(8,128)(2,1)} %bitcast.43) | data formatting | bytes 16777216 | tf_op jit(solution)/shard_map/mul | solution.py:24
  214.4 100.3 %bitcast_multiply_fusion = f32[2048,2304]{1,0:T(8,128)} fusion(bf16[16,4,128,2304]{3,2,1,0:T(8,128)(2,1)} %bitcast.49, bf16[2048,4,16]{0,2,1:T(8,128)(2,1)S(1)} %mul.51, bf16[2048,128,16]{1,0,2:T(8,128)(2,1)} %copy.10, f32[]{:T(128)S(6)} %convert_element_type.30), kind=kOutput, calls=%fused_computation.5 | convolution fusion | flops 77330907136 | bytes 65273860 | tf_op jit(solution)/shard_map/qptgbc,qgbcd->qptd/dot_general | solution.py:25
  314.6 314.1 %reduce-scatter.2.cloned.1.call-done = f32[512,2304]{1,0:T(8,128)} async-done(((f32[2048,2304]{1,0:T(8,128)}), f32[512,2304]{1,0:T(8,128)}) %reduce-scatter.2.cloned.1.call-update) | async-done | bytes 4718608 | tf_op jit(solution)/shard_map/reduce_scatter | solution.py:59
  628.7 4.0 convert_bitcast_fusion
  (20 shorter events, 1.8 us)
Async XLA Ops:
  7.2 77.9 %all-gather.2.cloned.1.call-start = ((), (), s32[]{:S(2)}) async-start(), calls=%async_computation.1 | async-start | bytes 3145728 | tf_op jit(solution)/shard_map/all_gather | solution.py:50
  34.4 103.3 %copy-start.3 = (s32[1,32,16]{1,2,0:T(8,128)S(1)}, s32[1,32,16]{1,2,0:T(8,128)}, u32[]{:S(2)}) copy-start(s32[1,32,16]{1,2,0:T(8,128)} %param.9) | copy-start | bytes 6148
  49.1 579.6 %reduce-scatter.2.cloned.1.call-start = ((), (), s32[]{:S(2)}) async-start(), calls=%async_computation.2 | async-start | bytes 23592960 | tf_op jit(solution)/shard_map/reduce_scatter | solution.py:59
  85.1 98.9 %copy-start = (bf16[512,2048]{1,0:T(8,128)(2,1)S(1)}, bf16[512,2048]{1,0:T(8,128)(2,1)}, u32[]{:S(2)}) copy-start(bf16[512,2048]{1,0:T(8,128)(2,1)} %all-gather.2.cloned.1.call-done) | copy-start | bytes 6291460
  85.1 25.7 %collective-permute-start = (bf16[512,2048]{1,0:T(8,128)(2,1)}, bf16[512,2048]{1,0:T(8,128)(2,1)S(1)}, u32[]{:S(2)}, u32[]{:S(2)}) collective-permute-start(bf16[512,2048]{1,0:T(8,128)(2,1)} %all-gather.2.cloned.1.call-done), channel_id=1, source_target_pairs={{0,2},{2,4},{4,6},{6,0},{1,3},{3,5},{5,7},{7,1},{8,10},{10,12},{12... | collective-permute-start | bytes 6291464 | tf_op jit(solution)/shard_map/ppermute | solution.py:16
  110.8 1.3 copy-start.1
  112.1 25.6 %collective-permute-start.1 = (bf16[512,2048]{1,0:T(8,128)(2,1)S(1)}, bf16[512,2048]{1,0:T(8,128)(2,1)}, u32[]{:S(2)}, u32[]{:S(2)}) collective-permute-start(bf16[512,2048]{1,0:T(8,128)(2,1)S(1)} %collective-permute-done), channel_id=1, source_target_pairs={{0,2},{2,4},{4,6},{6,0},{1,3},{3,5},{5,7},{7,1},{8,10},{10,12},{12... | collective-permute-start | bytes 6291464 | tf_op jit(solution)/shard_map/ppermute | solution.py:16
  137.6 25.8 %collective-permute-start.2 = (bf16[512,2048]{1,0:T(8,128)(2,1)}, bf16[512,2048]{1,0:T(8,128)(2,1)}, u32[]{:S(2)}, u32[]{:S(2)}) collective-permute-start(bf16[512,2048]{1,0:T(8,128)(2,1)} %collective-permute-done.1), channel_id=1, source_target_pairs={{0,2},{2,4},{4,6},{6,0},{1,3},{3,5},{5,7},{7,1},{8,10},{10,12},{12... | collective-permute-start | bytes 6291464 | tf_op jit(solution)/shard_map/ppermute | solution.py:16
  138.5 44.0 %copy-start.2 = (bf16[512,2048]{1,0:T(8,128)(2,1)S(1)}, bf16[512,2048]{1,0:T(8,128)(2,1)}, u32[]{:S(2)}) copy-start(bf16[512,2048]{1,0:T(8,128)(2,1)} %copy-done.1) | copy-start | bytes 6291460
Sparse Core Ops, SparseCore 0:
  49.2 35.8 all-gather.1
  314.8 313.9 reduce-scatter.1
